TPU v7x, 32 devices: a whole 2x2x4 slice. The times are simulated.
32 devices in a mesh: face: 4 (over z), strip: 8 (over y, x, core).
Axes of the slice: x: 2, y: 2, z: 4, core: 2. Of those that a mesh axis runs over, the one named last changes fastest.
Arguments:
- pixels_in: bfloat16 [4, 8, 64, 1024], P('face', 'strip'), may hold values from -6 to 6
- w_qkv: bfloat16 [1024, 3072], P(None, 'face'), may hold values from -0.1875 to 0.1875
- w_gate: bfloat16 [1024, 32], P(None, 'face'), may hold values from -0.1875 to 0.1875
- decay_rate: float32 [16], replicated, may hold values from 0.0005859375 to 0.05
- beta_bias: float32 [16], replicated, may hold values from -4 to 1
Outputs:
- mixed: bfloat16 [4, 8, 64, 1024], P('face', 'strip')
All inputs are finite; a program needn't handle non-finite values.
Results may differ from a plain program's by a relative error of at most 0.0069.
Values may be sent and summed in bfloat16 or wider, within the bound.
A program may use at most 192 MiB of HBM per device.

v0:
```python
import jax
import jax.numpy as jnp
from jax import lax
from jax.sharding import PartitionSpec as P

highest = lax.Precision.HIGHEST


def carried_in(part, axis, combine, identity):
    place = lax.axis_index(axis)
    gathered = jax.tree.map(lambda a: lax.all_gather(a, axis), part)
    state = jax.tree.map(lambda a, e: jnp.zeros_like(a) + jnp.asarray(e, a.dtype), part, identity)

    def one(turn, state):
        return combine(
            state, jax.tree.map(lambda a: lax.dynamic_index_in_dim(a, turn, 0, False), gathered)
        )

    return lax.fori_loop(0, place, one, state)


def unit_rows(tensor):
    return tensor / jnp.sqrt(jnp.sum(tensor * tensor, axis=-1, keepdims=True) + 1e-06)


def head_norm(tensor):
    normed = tensor / jnp.sqrt(jnp.mean(tensor * tensor, axis=-1, keepdims=True) + 1e-06)
    return normed.reshape(tensor.shape[0], -1)


def project(flat_px, w_full, gate_full):
    projected = jnp.dot(flat_px, w_full, preferred_element_type=jnp.float32).astype(jnp.bfloat16)
    gate_logits = jnp.dot(flat_px, gate_full, preferred_element_type=jnp.float32).astype(
        jnp.bfloat16
    )
    return (projected, gate_logits)


def unpack(projected, gate_logits, decay_rate, beta_bias):
    heads = decay_rate.shape[0]
    count = projected.shape[0]
    parts = projected.astype(jnp.float32).reshape(count, 3, heads, -1)
    logits = gate_logits.astype(jnp.float32)
    log_decay = -decay_rate[None, :] * jnp.exp(logits[:, :heads])
    strength = jax.nn.sigmoid(logits[:, heads:] + beta_bias[None, :])
    return (unit_rows(parts[:, 0]), unit_rows(parts[:, 1]), parts[:, 2], log_decay, strength)


def group_terms(queries, key_rows, val_rows, log_decay, strength):
    span = queries.shape[1]
    width = queries.shape[2]
    cumulative = jnp.cumsum(log_decay, axis=1)
    gap_log = cumulative[:, :, None] - cumulative[:, None, :]
    row_ids = lax.broadcasted_iota(jnp.int32, (span, span), 0)
    col_ids = lax.broadcasted_iota(jnp.int32, (span, span), 1)
    inclusive = row_ids >= col_ids
    strict = row_ids > col_ids
    within = jnp.where(inclusive, jnp.exp(jnp.where(inclusive, gap_log, 0.0)), 0.0)
    key_dot = jnp.einsum("hck,hjk->hcj", key_rows, key_rows, precision=highest)
    lower_part = jnp.where(strict, within * key_dot, 0.0) * strength[:, :, None]
    system = lower_part + jnp.eye(span, dtype=queries.dtype)
    scale_all = jnp.exp(cumulative)
    rhs_values = val_rows * strength[:, :, None]
    rhs_keys = key_rows * (strength * scale_all)[:, :, None]
    solved = lax.linalg.triangular_solve(
        system,
        jnp.concatenate([rhs_values, rhs_keys], axis=-1),
        left_side=True,
        lower=True,
        unit_diagonal=True,
    )
    new_values = solved[..., :width]
    mixing = solved[..., width:]
    scores = jnp.where(
        inclusive, within * jnp.einsum("hck,hjk->hcj", queries, key_rows, precision=highest), 0.0
    )
    tail_decay = jnp.exp(cumulative[:, -1:] - cumulative)
    weighted_keys = key_rows * tail_decay[:, :, None]
    end_scale = jnp.exp(cumulative[:, -1])
    transition = end_scale[:, None, None] * jnp.eye(width, dtype=queries.dtype) - jnp.einsum(
        "hck,hcj->hkj", mixing, weighted_keys, precision=highest
    )
    writes = jnp.einsum("hcv,hck->hvk", new_values, weighted_keys, precision=highest)
    effective_query = queries * scale_all[:, :, None] - jnp.einsum(
        "hcj,hjk->hck", scores, mixing, precision=highest
    )
    local_out = jnp.einsum("hcj,hjv->hcv", scores, new_values, precision=highest)
    return (local_out, effective_query, transition, writes)


def to_blocks(queries, key_rows, val_rows, log_decay, strength):
    count = queries.shape[0] // 64

    def shape_four(tensor):
        return tensor.reshape(count, 64, tensor.shape[1], tensor.shape[2]).transpose(0, 2, 1, 3)

    def shape_three(tensor):
        return tensor.reshape(count, 64, tensor.shape[1]).transpose(0, 2, 1)

    return (
        shape_four(queries),
        shape_four(key_rows),
        shape_four(val_rows),
        shape_three(log_decay),
        shape_three(strength),
    )


def from_blocks(outputs):
    count, heads, span, width = outputs.shape
    return outputs.transpose(0, 2, 1, 3).reshape(count * span, heads, width)


def carried(prefix, local_state, eye_block, zero_state):

    def compose(earlier, later):
        joined_map = jnp.einsum("hkj,hjl->hkl", earlier[0], later[0], precision=highest)
        joined_state = (
            jnp.einsum("hvk,hkj->hvj", earlier[1], later[0], precision=highest) + later[1]
        )
        return (joined_map, joined_state)

    _, incoming = carried_in((prefix, local_state), "strip", compose, (eye_block, zero_state))
    return incoming


def strip_scan(queries, key_rows, val_rows, log_decay, strength):
    blocks = to_blocks(queries, key_rows, val_rows, log_decay, strength)
    heads = queries.shape[1]
    width = queries.shape[2]
    eye_block = jnp.broadcast_to(jnp.eye(width, dtype=jnp.float32), (heads, width, width))
    zero_state = jnp.zeros((heads, width, width), jnp.float32)

    def advance_local(carry, block_in):
        carry_state, prefix = carry
        local_out, effective_query, transition, writes = group_terms(*block_in)
        outputs = local_out + jnp.einsum(
            "hck,hvk->hcv", effective_query, carry_state, precision=highest
        )
        lifted = jnp.einsum("hck,hjk->hcj", effective_query, prefix, precision=highest)
        carry_state = (
            jnp.einsum("hvk,hkj->hvj", carry_state, transition, precision=highest) + writes
        )
        prefix = jnp.einsum("hkj,hjl->hkl", prefix, transition, precision=highest)
        return ((carry_state, prefix), (outputs, lifted))

    (local_state, prefix), (outputs, lifted) = lax.scan(
        advance_local, (zero_state, eye_block), blocks
    )
    incoming = carried(prefix, local_state, eye_block, zero_state)
    outputs = outputs + jnp.einsum("nhcj,hvj->nhcv", lifted, incoming, precision=highest)
    return from_blocks(outputs)


def on_device(pixels_in, w_qkv, w_gate, decay_rate, beta_bias):
    w_full, gate_full = (
        lax.all_gather(w_qkv, "face", axis=1, tiled=True),
        lax.all_gather(w_gate, "face", axis=1, tiled=True),
    )
    rows_here = pixels_in.shape[1]
    width_cols = pixels_in.shape[2]
    features = pixels_in.shape[3]
    n_strip = lax.axis_size("strip")
    cols_here = width_cols // n_strip
    tall_rows = rows_here * n_strip
    plane = pixels_in.reshape(rows_here, width_cols, features)
    projected, gate_logits = project(
        plane.reshape(rows_here * width_cols, features), w_full, gate_full
    )
    row_out = strip_scan(*unpack(projected, gate_logits, decay_rate, beta_bias))
    arrived_proj, arrived_gates = (
        lax.all_to_all(
            projected.reshape(rows_here, width_cols, -1),
            "strip",
            split_axis=1,
            concat_axis=0,
            tiled=True,
        ),
        lax.all_to_all(
            gate_logits.reshape(rows_here, width_cols, -1),
            "strip",
            split_axis=1,
            concat_axis=0,
            tiled=True,
        ),
    )
    col_proj = arrived_proj.swapaxes(0, 1).reshape(tall_rows * cols_here, -1)
    col_gates = arrived_gates.swapaxes(0, 1).reshape(tall_rows * cols_here, -1)
    col_out = strip_scan(*unpack(col_proj, col_gates, decay_rate, beta_bias))
    col_mixed = head_norm(col_out).astype(jnp.bfloat16)
    col_tall = col_mixed.reshape(cols_here, tall_rows, -1).swapaxes(0, 1)
    returned = lax.all_to_all(col_tall, "strip", split_axis=0, concat_axis=1, tiled=True)
    row_mixed = head_norm(row_out).reshape(rows_here, width_cols, -1)
    mixed = (row_mixed + returned.astype(jnp.float32)).astype(jnp.bfloat16)
    return mixed[None]


def solution(mesh):
    in_specs = (P("face", "strip", None, None), P(None, "face"), P(None, "face"), P(), P())
    out_specs = P("face", "strip", None, None)
    return jax.shard_map(
        on_device, mesh=mesh, in_specs=in_specs, out_specs=out_specs, check_vma=False
    )
```

profile of v0, /device:TPU:0, one launch (start us, length us, event | category | flops | bytes accessed | tf_op | source)
XLA Modules:
  0.0 444.6 jit_solution(4246070837941400303)
XLA Ops:
  7.3 15.1 %all_gather.30 = bf16[1024,32]{0,1:T(8,128)(2,1)S(1)} all-gather(bf16[1024,8]{0,1:T(8,128)(2,1)} %param.13), channel_id=1, replica_groups=mesh['face'=4,'strip'=8] {'face'}, dimensions={1}, use_global_device_ids=true | all-gather | bytes 81920 | tf_op jit(solution)/shard_map/all_gather | solution.py:158
  24.7 3.7 all-to-all-start
  29.4 3.8 all-to-all-done
  35.7 91.3 %all-gather.10.cloned.1.call-done = bf16[1024,3072]{1,0:T(8,128)(2,1)} async-done(((bf16[1024,768]{1,0:T(8,128)(2,1)}), bf16[1024,3072]{1,0:T(8,128)(2,1)}) %all-gather.10.cloned.1.call-update) | async-done | bytes 6291472 | tf_op jit(solution)/shard_map/all_gather | solution.py:157
  127.0 4.0 convolution_convert_fusion
  134.1 78.6 %custom-call.4 = f32[16,1,64,64]{2,3,1,0:T(8,128)S(1)} custom-call(f32[16,1,64,64]{3,2,1,0:T(8,128)S(1)} %fusion.19), custom_call_target="InvertDiagBlocksLowerTriangular" | custom-call | tf_op jit(solution)/shard_map/while/body/eval_jaxpr/triangular_solve/custom-call.1 | solution.py:65
  214.4 1.4 convolution_subtract_fusion.2
  215.8 1.4 fusion.67
  218.2 2.1 convolution_add_fusion.2
  220.9 3.0 reduce.11
  224.9 3.6 all-to-all-start.1
  229.7 7.1 %all-to-all-done.1 = bf16[8,2,12288]{2,1,0:T(2,128)(2,1)S(1)} async-done(((bf16[8,2,12288]{2,1,0:T(2,128)(2,1)}), bf16[8,2,12288]{2,1,0:T(2,128)(2,1)S(1)}, u32[]{:S(2)}, u32[]{:S(2)}) %all-to-all-start.1) | async-done | bytes 393248 | tf_op jit(solution)/shard_map/all_to_all | solution.py:172
  240.5 2.2 fusion.23
  242.7 79.3 %custom-call.5 = f32[16,1,64,64]{2,3,1,0:T(8,128)} custom-call(f32[16,1,64,64]{3,2,1,0:T(8,128)S(1)} %fusion.23), custom_call_target="InvertDiagBlocksLowerTriangular" | custom-call | tf_op jit(solution)/shard_map/while/body/eval_jaxpr/triangular_solve/custom-call.1 | solution.py:65
  322.5 2.2 fusion.31
  324.8 1.4 convolution_subtract_fusion
  331.3 1.9 convolution_subtract_fusion.3
  333.8 2.1 convolution_add_fusion
  336.9 1.7 fusion.65
  344.4 2.1 fusion.41
  346.7 17.2 %all-gather.16.cloned.1.call-done = f32[128,64,64]{2,1,0:T(8,128)} async-done(((f32[16,64,64]{2,1,0:T(8,128)}), f32[128,64,64]{2,1,0:T(8,128)}) %all-gather.16.cloned.1.call-update) | async-done | bytes 2097168 | tf_op jit(solution)/shard_map/all_gather | solution.py:11
  363.9 38.3 %all-gather.18.cloned.1.call-done = f32[128,64,64]{2,1,0:T(8,128)} async-done(((f32[16,64,64]{2,1,0:T(8,128)}), f32[128,64,64]{2,1,0:T(8,128)}) %all-gather.18.cloned.1.call-update) | async-done | bytes 2097168 | tf_op jit(solution)/shard_map/all_gather | solution.py:11
  405.1 26.5 %all-to-all-start.2 = ((bf16[8,8,1024]{2,1,0:T(8,128)(2,1)}), bf16[8,8,1024]{2,1,0:T(8,128)(2,1)S(1)}, u32[]{:S(2)}, u32[]{:S(2)}) async-start(bf16[8,8,1024]{2,1,0:T(8,128)(2,1)} %copy.134), calls=%async_computation.2 | async-start | bytes 262144 | tf_op jit(solution)/shard_map/all_to_all | solution.py:192
  432.1 5.0 %all-to-all-done.2 = bf16[8,8,1024]{2,1,0:T(8,128)(2,1)S(1)} async-done(((bf16[8,8,1024]{2,1,0:T(8,128)(2,1)}), bf16[8,8,1024]{2,1,0:T(8,128)(2,1)S(1)}, u32[]{:S(2)}, u32[]{:S(2)}) %all-to-all-start.2) | async-done | bytes 131104 | tf_op jit(solution)/shard_map/all_to_all | solution.py:192
  (132 shorter events, 35.3 us)
Async XLA Ops:
  6.5 15.9 %copy-start = (bf16[1,1,64,1024]{3,2,1,0:T(8,128)(2,1)S(1)}, bf16[1,1,64,1024]{3,2,1,0:T(8,128)(2,1)}, u32[]{:S(2)}) copy-start(bf16[1,1,64,1024]{3,2,1,0:T(8,128)(2,1)} %param.11) | copy-start | bytes 393220
  6.5 120.5 %all-gather.10.cloned.1.call-start = ((), (), s32[]{:S(2)}) async-start(), calls=%async_computation.3 | async-start | bytes 7864320 | tf_op jit(solution)/shard_map/all_gather | solution.py:157
  24.7 8.4 %all-to-all-start = ((bf16[8,2,128]{2,1,0:T(2,128)(2,1)}), bf16[8,2,128]{2,1,0:T(2,128)(2,1)S(1)}, u32[]{:S(2)}, u32[]{:S(2)}) async-start(bf16[8,2,128]{2,1,0:T(2,128)(2,1)} %reshape.328), calls=%async_computation | async-start | bytes 8192 | tf_op jit(solution)/shard_map/all_to_all | solution.py:179
  28.5 315.7 %all-gather.12.cloned.1.call-start = ((), (), s32[]{:S(2)}) async-start(), calls=%async_computation.4 | async-start | bytes 4718592 | tf_op jit(solution)/shard_map/all_gather | solution.py:11
  28.5 104.1 %copy-start.14 = (pred[64,64]{1,0:T(8,128)(4,1)}, pred[64,64]{1,0:T(8,128)(4,1)S(1)}, u32[]{:S(2)}) copy-start(pred[64,64]{1,0:T(8,128)(4,1)S(1)} %get-tuple-element.250) | copy-start | bytes 12292
  28.6 187.3 %copy-start.7 = (f32[64,64]{1,0:T(8,128)}, f32[64,64]{1,0:T(8,128)S(1)}, u32[]{:S(2)}) copy-start(f32[64,64]{1,0:T(8,128)S(1)} %get-tuple-element.251) | copy-start | bytes 49156
  28.6 104.0 %copy-start.19 = (pred[64,64]{1,0:T(8,128)(4,1)}, pred[64,64]{1,0:T(8,128)(4,1)S(1)}, u32[]{:S(2)}) copy-start(pred[64,64]{1,0:T(8,128)(4,1)S(1)} %get-tuple-element.248) | copy-start | bytes 12292
  28.7 104.0 %copy-start.20 = (pred[64,64]{1,0:T(8,128)(4,1)}, pred[64,64]{1,0:T(8,128)(4,1)S(1)}, u32[]{:S(2)}) copy-start(pred[64,64]{1,0:T(8,128)(4,1)S(1)} %get-tuple-element.249) | copy-start | bytes 12292
  28.7 104.0 %copy-start.13 = (f32[64,64]{1,0:T(8,128)}, f32[64,64]{1,0:T(8,128)S(1)}, u32[]{:S(2)}) copy-start(f32[64,64]{1,0:T(8,128)S(1)} %fusion.79) | copy-start | bytes 49156
  132.7 85.5 %copy-start.11 = (f32[64,16]{0,1:T(8,128)}, f32[64,16]{0,1:T(8,128)S(1)}, u32[]{:S(2)}) copy-start(f32[64,16]{0,1:T(8,128)S(1)} %add_sqrt_fusion.4) | copy-start | bytes 12292
  217.2 126.9 %all-gather.14.cloned.1.call-start = ((), (), s32[]{:S(2)}) async-start(), calls=%async_computation.5 | async-start | bytes 4718592 | tf_op jit(solution)/shard_map/all_gather | solution.py:11
  224.9 11.9 %all-to-all-start.1 = ((bf16[8,2,12288]{2,1,0:T(2,128)(2,1)}), bf16[8,2,12288]{2,1,0:T(2,128)(2,1)S(1)}, u32[]{:S(2)}, u32[]{:S(2)}) async-start(bf16[8,2,12288]{2,1,0:T(2,128)(2,1)} %reshape.330), calls=%async_computation.1 | async-start | bytes 786432 | tf_op jit(solution)/shard_map/all_to_all | solution.py:172
  228.6 135.3 %all-gather.16.cloned.1.call-start = ((), (), s32[]{:S(2)}) async-start(), calls=%async_computation.6 | async-start | bytes 4718592 | tf_op jit(solution)/shard_map/all_gather | solution.py:11
  240.2 81.8 %copy-start.6 = (f32[64,1,16,64]{3,2,1,0:T(8,128)S(1)}, f32[64,1,16,64]{3,2,1,0:T(8,128)}, u32[]{:S(2)}) copy-start(f32[64,1,16,64]{3,2,1,0:T(8,128)} %get-tuple-element.220) | copy-start | bytes 786436
  240.3 81.8 %copy-start.9 = (f32[16,64]{1,0:T(8,128)S(1)}, f32[16,64]{1,0:T(8,128)}, u32[]{:S(2)}) copy-start(f32[16,64]{1,0:T(8,128)} %get-tuple-element.234) | copy-start | bytes 12292
  240.3 81.8 %copy-start.10 = (f32[16,64]{1,0:T(8,128)S(1)}, f32[16,64]{1,0:T(8,128)}, u32[]{:S(2)}) copy-start(f32[16,64]{1,0:T(8,128)} %get-tuple-element.235) | copy-start | bytes 12292
  240.3 84.5 %copy-start.8 = (f32[64,64]{1,0:T(8,128)S(1)}, f32[64,64]{1,0:T(8,128)}, u32[]{:S(2)}) copy-start(f32[64,64]{1,0:T(8,128)} %copy-done.7) | copy-start | bytes 49156
  240.3 84.5 %copy-start.17 = (f32[16,64]{1,0:T(8,128)S(1)}, f32[16,64]{1,0:T(8,128)}, u32[]{:S(2)}) copy-start(f32[16,64]{1,0:T(8,128)} %get-tuple-element.233) | copy-start | bytes 12292
  240.3 84.5 %copy-start.21 = (f32[16]{0:T(128)S(1)}, f32[16]{0:T(128)}, u32[]{:S(2)}) copy-start(f32[16]{0:T(128)} %exp.84) | copy-start | bytes 196
  242.7 85.9 %copy-start.3 = (f32[64,1,16,64]{3,2,1,0:T(8,128)S(1)}, f32[64,1,16,64]{3,2,1,0:T(8,128)}, u32[]{:S(2)}) copy-start(f32[64,1,16,64]{3,2,1,0:T(8,128)} %get-tuple-element.225) | copy-start | bytes 786436
  322.0 6.9 %copy-start.12 = (f32[64,16]{0,1:T(8,128)S(1)}, f32[64,16]{0,1:T(8,128)}, u32[]{:S(2)}) copy-start(f32[64,16]{0,1:T(8,128)} %copy-done.11) | copy-start | bytes 12292
  322.0 6.9 %copy-start.15 = (pred[64,64]{1,0:T(8,128)(4,1)S(1)}, pred[64,64]{1,0:T(8,128)(4,1)}, u32[]{:S(2)}) copy-start(pred[64,64]{1,0:T(8,128)(4,1)} %copy-done.14) | copy-start | bytes 12292
  328.4 73.9 %all-gather.18.cloned.1.call-start = ((), (), s32[]{:S(2)}) async-start(), calls=%async_computation.7 | async-start | bytes 4718592 | tf_op jit(solution)/shard_map/all_gather | solution.py:11
  405.1 32.0 %all-to-all-start.2 = ((bf16[8,8,1024]{2,1,0:T(8,128)(2,1)}), bf16[8,8,1024]{2,1,0:T(8,128)(2,1)S(1)}, u32[]{:S(2)}, u32[]{:S(2)}) async-start(bf16[8,8,1024]{2,1,0:T(8,128)(2,1)} %copy.134), calls=%async_computation.2 | async-start | bytes 262144 | tf_op jit(solution)/shard_map/all_to_all | solution.py:192
  (6 other events, 23.6 us)
Sparse Core Ops, SparseCore 0:
  8.9 118.0 all-gather.9
  217.4 39.1 all-gather.11
  258.4 37.3 all-gather.13
  328.5 35.3 all-gather.15
  365.7 36.5 all-gather.17
where the time goes:
time: 453 us; the launch traced here: 445 us
  other arithmetic  168 us (37%)
  waiting for transfers between devices  164 us (36%)
  matrix products  37.2 us (8%)
  starting transfers between devices  35 us (8%)
  blocking collectives  15.1 us (3%)
  between operations  14 us (3%)
  local copies, waits for them, and re-layouts  11.4 us (3%)
    another operation x5, other arithmetic, group_terms(): lax.linalg.triangular_solve(system, jnp.concatenate([rhs_values, rhs_keys...  158 us
    all_gather x1, waiting for transfers between devices, on_device(): lax.all_gather(w_qkv, 'face', axis=1, tiled=True)  91.3 us
    all_gather x4, waiting for transfers between devices, carried_in(): gathered = jax.tree.map(lambda a: lax.all_gather(a, axis), part)  55.6 us
    all_to_all x1, starting transfers between devices, on_device(): lax.all_to_all(col_tall, 'strip', split_axis=0, concat_axis=1, tiled=True)  26.5 us
    all_gather x1, blocking collectives, on_device(): lax.all_gather(w_gate, 'face', axis=1, tiled=True)  15.1 us
  transfers between devices with their start and end apart: 8, of which 6 were waited for; matrix products, arithmetic and copies ran while one was open for 27% of the time, Pallas kernels for 0%

commit v1 on v0

--- a/solution.py
+++ b/solution.py
@@ -1,9 +1,21 @@
+import functools
 import jax
 import jax.numpy as jnp
 from jax import lax
 from jax.sharding import PartitionSpec as P
+from jax.lax import all_to_all, axis_size
 
 highest = lax.Precision.HIGHEST
+
+
+def touch_ladders(own_rows, which_axis):
+    items = []
+    for _ in range(axis_size(which_axis)):
+        items.append(own_rows)
+    return jnp.concatenate(all_to_all(jnp.stack(items), which_axis, 0, 0), axis=1)
+
+
+try_all_the_wall = functools.partial(touch_ladders, which_axis="face")
 
 
 def carried_in(part, axis, combine, identity):
@@ -154,7 +166,7 @@
 
 def on_device(pixels_in, w_qkv, w_gate, decay_rate, beta_bias):
     w_full, gate_full = (
-        lax.all_gather(w_qkv, "face", axis=1, tiled=True),
+        try_all_the_wall(w_qkv),
         lax.all_gather(w_gate, "face", axis=1, tiled=True),
     )
     rows_here = pixels_in.shape[1]

time: 453 us -> 508 us (1.12)
  waiting for transfers between devices: 164 us -> 208 us
  local copies, waits for them, and re-layouts: 11.4 us -> 16.6 us
    all_to_all x0 -> x1, waiting for transfers between devices: none -> 136 us  [touch_ladders(): all_to_all(jnp.stack(items), which_axis, 0, 0)]
    all_gather x1 -> x0, waiting for transfers between devices: 91.3 us -> none  [on_device(): lax.all_gather(w_qkv, 'face', axis=1, tiled=True)]
    all_to_all x0 -> x1, starting transfers between devices: none -> 5.38 us  [touch_ladders(): all_to_all(jnp.stack(items), which_axis, 0, 0)]
  transfers between devices with their start and end apart: 8 -> 8, of which waited for: 6 -> 6; matrix products, arithmetic and copies ran while one was open for 27% -> 24% of each run, Pallas kernels for 0% -> 0%
where the time goes in v1:
time: 508 us; the launch traced here: 498 us
  waiting for transfers between devices  208 us (41%)
  other arithmetic  167 us (33%)
  starting transfers between devices  39.6 us (8%)
  matrix products  36.8 us (7%)
  local copies, waits for them, and re-layouts  16.6 us (3%)
  blocking collectives  15.3 us (3%)
  between operations  14.3 us (3%)
    another operation x5, other arithmetic, group_terms(): lax.linalg.triangular_solve(system, jnp.concatenate([rhs_values, rhs_keys...  157 us
    all_to_all x1, waiting for transfers between devices, touch_ladders(): all_to_all(jnp.stack(items), which_axis, 0, 0)  136 us
    all_gather x4, waiting for transfers between devices, carried_in(): gathered = jax.tree.map(lambda a: lax.all_gather(a, axis), part)  56.4 us
    all_to_all x1, starting transfers between devices, on_device(): lax.all_to_all(col_tall, 'strip', split_axis=0, concat_axis=1, tiled=True)  26.5 us
    all_gather x1, blocking collectives, on_device(): lax.all_gather(w_gate, 'face', axis=1, tiled=True)  15.3 us
  transfers between devices with their start and end apart: 8, of which 6 were waited for; matrix products, arithmetic and copies ran while one was open for 24% of the time, Pallas kernels for 0%

profile of v1, /device:TPU:0, one launch (start us, length us, event | category | flops | bytes accessed | tf_op | source)
XLA Modules:
  0.0 498.2 jit_solution(10281778399850468841)
XLA Ops:
  6.5 15.3 %all_gather.27 = bf16[1024,32]{0,1:T(8,128)(2,1)S(1)} all-gather(bf16[1024,8]{0,1:T(8,128)(2,1)} %param.13), channel_id=1, replica_groups=mesh['face'=4,'strip'=8] {'face'}, dimensions={1}, use_global_device_ids=true | all-gather | bytes 81920 | tf_op jit(solution)/shard_map/all_gather | solution.py:170
  24.1 3.7 all-to-all-start.1
  27.8 1.7 copy.102
  29.6 2.9 all-to-all-done.1
  32.5 3.4 stack.2
  35.9 5.4 %all-to-all-start = ((bf16[4,1024,768]{1,2,0:T(8,128)(2,1)}), bf16[4,1024,768]{1,2,0:T(8,128)(2,1)}, u32[]{:S(2)}, u32[]{:S(2)}) async-start(bf16[4,1024,768]{1,2,0:T(8,128)(2,1)} %stack.2), calls=%async_computation | async-start | bytes 12582912 | tf_op jit(solution)/shard_map/all_to_all | solution.py:15
  43.5 136.2 %all-to-all-done = bf16[4,1024,768]{1,2,0:T(8,128)(2,1)} async-done(((bf16[4,1024,768]{1,2,0:T(8,128)(2,1)}), bf16[4,1024,768]{1,2,0:T(8,128)(2,1)}, u32[]{:S(2)}, u32[]{:S(2)}) %all-to-all-start) | async-done | bytes 6291488 | tf_op jit(solution)/shard_map/all_to_all | solution.py:15
  179.7 4.8 convolution_convert_fusion
  187.6 78.6 %custom-call.4 = f32[16,1,64,64]{2,3,1,0:T(8,128)S(1)} custom-call(f32[16,1,64,64]{3,2,1,0:T(8,128)S(1)} %fusion.19), custom_call_target="InvertDiagBlocksLowerTriangular" | custom-call | tf_op jit(solution)/shard_map/while/body/eval_jaxpr/triangular_solve/custom-call.1 | solution.py:77
  269.9 2.1 convolution_add_fusion.2
  274.3 3.0 reduce.11
  278.3 3.5 all-to-all-start.2
  282.4 7.9 %all-to-all-done.2 = bf16[8,2,12288]{2,1,0:T(2,128)(2,1)S(1)} async-done(((bf16[8,2,12288]{2,1,0:T(2,128)(2,1)}), bf16[8,2,12288]{2,1,0:T(2,128)(2,1)S(1)}, u32[]{:S(2)}, u32[]{:S(2)}) %all-to-all-start.2) | async-done | bytes 393248 | tf_op jit(solution)/shard_map/all_to_all | solution.py:184
  294.0 2.0 fusion.23
  296.1 78.6 %custom-call.5 = f32[16,1,64,64]{2,3,1,0:T(8,128)S(1)} custom-call(f32[16,1,64,64]{3,2,1,0:T(8,128)S(1)} %fusion.23), custom_call_target="InvertDiagBlocksLowerTriangular" | custom-call | tf_op jit(solution)/shard_map/while/body/eval_jaxpr/triangular_solve/custom-call.1 | solution.py:77
  376.4 1.4 convolution_subtract_fusion
  379.3 2.1 convolution_add_fusion
  387.6 1.7 fusion.65
  390.6 2.3 fusion.11
  397.2 2.1 fusion.41
  399.3 18.0 %all-gather.15.cloned.1.call-done = f32[128,64,64]{2,1,0:T(8,128)} async-done(((f32[16,64,64]{2,1,0:T(8,128)}), f32[128,64,64]{2,1,0:T(8,128)}) %all-gather.15.cloned.1.call-update) | async-done | bytes 2097168 | tf_op jit(solution)/shard_map/all_gather | solution.py:23
  417.3 38.4 %all-gather.13.cloned.1.call-done = f32[128,64,64]{2,1,0:T(8,128)} async-done(((f32[16,64,64]{2,1,0:T(8,128)}), f32[128,64,64]{2,1,0:T(8,128)}) %all-gather.13.cloned.1.call-update) | async-done | bytes 2097168 | tf_op jit(solution)/shard_map/all_gather | solution.py:23
  458.5 26.5 %all-to-all-start.3 = ((bf16[8,8,1024]{2,1,0:T(8,128)(2,1)}), bf16[8,8,1024]{2,1,0:T(8,128)(2,1)S(1)}, u32[]{:S(2)}, u32[]{:S(2)}) async-start(bf16[8,8,1024]{2,1,0:T(8,128)(2,1)} %copy.137), calls=%async_computation.3 | async-start | bytes 262144 | tf_op jit(solution)/shard_map/all_to_all | solution.py:204
  485.7 4.8 all-to-all-done.3
  (137 shorter events, 37.3 us)
Async XLA Ops:
  6.5 15.3 %copy-start = (bf16[1,1,64,1024]{3,2,1,0:T(8,128)(2,1)S(1)}, bf16[1,1,64,1024]{3,2,1,0:T(8,128)(2,1)}, u32[]{:S(2)}) copy-start(bf16[1,1,64,1024]{3,2,1,0:T(8,128)(2,1)} %param.11) | copy-start | bytes 393220
  24.1 8.3 %all-to-all-start.1 = ((bf16[8,2,128]{2,1,0:T(2,128)(2,1)}), bf16[8,2,128]{2,1,0:T(2,128)(2,1)S(1)}, u32[]{:S(2)}, u32[]{:S(2)}) async-start(bf16[8,2,128]{2,1,0:T(2,128)(2,1)} %reshape.338), calls=%async_computation.1 | async-start | bytes 8192 | tf_op jit(solution)/shard_map/all_to_all | solution.py:191
  35.9 5.4 %copy-start.22 = (f32[16]{0:T(128)S(1)}, f32[16]{0:T(128)}, u32[]{:S(2)}) copy-start(f32[16]{0:T(128)} %param.14) | copy-start | bytes 196
  35.9 6.9 %copy-start.21 = (f32[16]{0:T(128)S(1)}, f32[16]{0:T(128)}, u32[]{:S(2)}) copy-start(f32[16]{0:T(128)} %param.15) | copy-start | bytes 196
  35.9 143.8 %all-to-all-start = ((bf16[4,1024,768]{1,2,0:T(8,128)(2,1)}), bf16[4,1024,768]{1,2,0:T(8,128)(2,1)}, u32[]{:S(2)}, u32[]{:S(2)}) async-start(bf16[4,1024,768]{1,2,0:T(8,128)(2,1)} %stack.2), calls=%async_computation | async-start | bytes 12582912 | tf_op jit(solution)/shard_map/all_to_all | solution.py:15
  41.3 355.6 %all-gather.11.cloned.1.call-start = ((), (), s32[]{:S(2)}) async-start(), calls=%async_computation.5 | async-start | bytes 4718592 | tf_op jit(solution)/shard_map/all_gather | solution.py:23
  41.4 144.8 %copy-start.11 = (f32[64,64]{1,0:T(8,128)}, f32[64,64]{1,0:T(8,128)S(1)}, u32[]{:S(2)}) copy-start(f32[64,64]{1,0:T(8,128)S(1)} %fusion.79) | copy-start | bytes 49156
  41.4 144.8 %copy-start.13 = (pred[64,64]{1,0:T(8,128)(4,1)}, pred[64,64]{1,0:T(8,128)(4,1)S(1)}, u32[]{:S(2)}) copy-start(pred[64,64]{1,0:T(8,128)(4,1)S(1)} %get-tuple-element.250) | copy-start | bytes 12292
  41.4 230.8 %copy-start.7 = (f32[64,64]{1,0:T(8,128)}, f32[64,64]{1,0:T(8,128)S(1)}, u32[]{:S(2)}) copy-start(f32[64,64]{1,0:T(8,128)S(1)} %get-tuple-element.251) | copy-start | bytes 49156
  41.5 144.7 %copy-start.18 = (pred[64,64]{1,0:T(8,128)(4,1)}, pred[64,64]{1,0:T(8,128)(4,1)S(1)}, u32[]{:S(2)}) copy-start(pred[64,64]{1,0:T(8,128)(4,1)S(1)} %get-tuple-element.248) | copy-start | bytes 12292
  41.5 144.7 %copy-start.20 = (pred[64,64]{1,0:T(8,128)(4,1)}, pred[64,64]{1,0:T(8,128)(4,1)S(1)}, u32[]{:S(2)}) copy-start(pred[64,64]{1,0:T(8,128)(4,1)S(1)} %get-tuple-element.249) | copy-start | bytes 12292
  272.0 124.9 %all-gather.9.cloned.1.call-start = ((), (), s32[]{:S(2)}) async-start(), calls=%async_computation.4 | async-start | bytes 4718592 | tf_op jit(solution)/shard_map/all_gather | solution.py:23
  278.3 12.0 %all-to-all-start.2 = ((bf16[8,2,12288]{2,1,0:T(2,128)(2,1)}), bf16[8,2,12288]{2,1,0:T(2,128)(2,1)S(1)}, u32[]{:S(2)}, u32[]{:S(2)}) async-start(bf16[8,2,12288]{2,1,0:T(2,128)(2,1)} %reshape.340), calls=%async_computation.2 | async-start | bytes 786432 | tf_op jit(solution)/shard_map/all_to_all | solution.py:184
  281.7 135.6 %all-gather.15.cloned.1.call-start = ((), (), s32[]{:S(2)}) async-start(), calls=%async_computation.7 | async-start | bytes 4718592 | tf_op jit(solution)/shard_map/all_gather | solution.py:23
  292.6 82.2 %copy-start.9 = (f32[16,64]{1,0:T(8,128)S(1)}, f32[16,64]{1,0:T(8,128)}, u32[]{:S(2)}) copy-start(f32[16,64]{1,0:T(8,128)} %get-tuple-element.234) | copy-start | bytes 12292
  293.7 81.0 %copy-start.6 = (f32[64,1,16,64]{3,2,1,0:T(8,128)S(1)}, f32[64,1,16,64]{3,2,1,0:T(8,128)}, u32[]{:S(2)}) copy-start(f32[64,1,16,64]{3,2,1,0:T(8,128)} %get-tuple-element.220) | copy-start | bytes 786436
  293.7 82.7 %copy-start.17 = (f32[16,64]{1,0:T(8,128)S(1)}, f32[16,64]{1,0:T(8,128)}, u32[]{:S(2)}) copy-start(f32[16,64]{1,0:T(8,128)} %get-tuple-element.233) | copy-start | bytes 12292
  293.7 82.7 %copy-start.23 = (f32[16]{0:T(128)S(1)}, f32[16]{0:T(128)}, u32[]{:S(2)}) copy-start(f32[16]{0:T(128)} %exp.84) | copy-start | bytes 196
  375.3 6.4 %copy-start.4 = (f32[64,1,16,64]{3,2,1,0:T(8,128)S(1)}, f32[64,1,16,64]{3,2,1,0:T(8,128)}, u32[]{:S(2)}) copy-start(f32[64,1,16,64]{3,2,1,0:T(8,128)} %get-tuple-element.225) | copy-start | bytes 786436
  381.4 74.3 %all-gather.13.cloned.1.call-start = ((), (), s32[]{:S(2)}) async-start(), calls=%async_computation.6 | async-start | bytes 4718592 | tf_op jit(solution)/shard_map/all_gather | solution.py:23
  387.6 6.4 %copy-start.5 = (f32[64,1,16,64]{3,2,1,0:T(8,128)S(1)}, f32[64,1,16,64]{3,2,1,0:T(8,128)}, u32[]{:S(2)}) copy-start(f32[64,1,16,64]{3,2,1,0:T(8,128)} %get-tuple-element.222) | copy-start | bytes 786436
  387.6 6.4 %copy-start.15 = (f32[16,64]{1,0:T(8,128)S(1)}, f32[16,64]{1,0:T(8,128)}, u32[]{:S(2)}) copy-start(f32[16,64]{1,0:T(8,128)} %get-tuple-element.232) | copy-start | bytes 12292
  455.7 35.5 %copy-start.1 = (bf16[1,1,64,1024]{3,2,1,0:T(8,128)(2,1)S(1)}, bf16[1,1,64,1024]{3,2,1,0:T(8,128)(2,1)}, u32[]{:S(2)}) copy-start(bf16[1,1,64,1024]{3,2,1,0:T(8,128)(2,1)} %param.11) | copy-start | bytes 393220
  458.5 32.0 %all-to-all-start.3 = ((bf16[8,8,1024]{2,1,0:T(8,128)(2,1)}), bf16[8,8,1024]{2,1,0:T(8,128)(2,1)S(1)}, u32[]{:S(2)}, u32[]{:S(2)}) async-start(bf16[8,8,1024]{2,1,0:T(8,128)(2,1)} %copy.137), calls=%async_computation.3 | async-start | bytes 262144 | tf_op jit(solution)/shard_map/all_to_all | solution.py:204
  (8 other events, 18.7 us)
Sparse Core Ops, SparseCore 0:
  272.1 38.1 all-gather.10
  312.2 37.3 all-gather.8
  381.5 35.7 all-gather.14
  419.1 36.5 all-gather.12
